TPU v7x, 32 devices: a whole 2x2x4 slice. The times are simulated.
32 devices in a mesh: scene: 2 (over y), aper: 8 (over z, x), range: 2 (over core).
Axes of the slice: x: 2, y: 2, z: 4, core: 2. Of those that a mesh axis runs over, the one named last changes fastest.
Arguments:
- images: bfloat16 [16, 2, 512, 256], P(('scene', 'aper'), None, None, 'range'), parts along dimension 0, may hold values from -6 to 6
- interp_matrix: bfloat16 [1024, 512], replicated, may hold values from -0.25 to 0.25
- offsets: int32 [3, 2, 1024], replicated, may hold values from -28 to 28, as said below
- tap_index: int32 [3, 2, 1024], replicated, may hold values from 0 to 15
- tap_table: float32 [16, 8], replicated, may hold values from -1.5 to 1.5
- phase_base: float32 [3, 2, 1024], replicated, may hold values from -3.140625 to 3.140625
- phase_slope: float32 [3, 2, 1024], replicated, may hold values from -0.5 to 0.5
Outputs:
- merged: bfloat16 [16, 2, 512, 256], P(('scene', 'aper'), None, None, 'range'), parts along dimension 0
There are 2 independent parts, one for each index of `scene`. A program takes and returns all parts, laid end to end along the dimension named above; an argument that names none is the same for every part. Nothing has to cross between parts.
Inputs may be any that keep to these rules, and one draw needn't show every extreme that they name: `offsets`: for every level and role both -28 and 28 occur.
All inputs are finite; a program needn't handle non-finite values.
Results may differ from a plain program's by a relative error of at most 0.0085.
Values may be sent and summed in bfloat16 or wider, within the bound.
A program may use at most 64 MiB of HBM per device.

v0:
```python
import functools

import jax
import jax.numpy as jnp
from jax import lax
from jax.experimental import pallas as pl
from jax.experimental.pallas import tpu as pltpu
from jax.sharding import PartitionSpec as P

MESH = pl.DeviceIdType.MESH
LANES = 128
REACH = 32
FINE = 8
SEND_LAG = 1
MERGE_LAG = 5
F32 = jnp.float32
BF16 = jnp.bfloat16


def sincos(angle):
    turns = jnp.floor(angle * 0.6366197723675814 + 0.5)
    rest = angle - turns * 1.5703125
    rest = rest - turns * 4.837512969970703125e-4
    rest = rest - turns * 7.54978995489188216e-8
    quadrant = turns.astype(jnp.int32)
    square = rest * rest
    sine = rest + rest * square * (
        -1.6666654611e-1 + square * (8.3321608736e-3 + square * -1.9515295891e-4)
    )
    cosine = (1.0 - 0.5 * square) + square * square * (
        4.166664568298827e-2 + square * (-1.388731625493765e-3 + square * 2.443315711809948e-5)
    )
    odd = (quadrant & 1) == 1
    swapped_sine = jnp.where(odd, cosine, sine)
    swapped_cosine = jnp.where(odd, sine, cosine)
    sine = jnp.where((quadrant & 2) == 2, -swapped_sine, swapped_sine)
    cosine = jnp.where(((quadrant + 1) & 2) == 2, -swapped_cosine, swapped_cosine)
    return sine, cosine


def kernel(
    levels,
    images,
    matrix,
    offsets,
    tap_index,
    tap_table,
    phase_base,
    phase_slope,
    out,
    image,
    rows_of,
    params,
    outgoing,
    incoming,
    kept,
    windows,
    merged,
    handed,
    local_sem,
    first_sem,
    inter_sem,
    merge_sem,
    last_sem,
):
    width = image.shape[2]
    angles = image.shape[3]
    span = images.shape[3]
    share = rows_of.shape[1]
    tiles = share // LANES
    steps = width // REACH
    per_owner = span // REACH
    taps = tap_table.shape[0]
    scene = lax.axis_index("scene")
    aper = lax.axis_index("aper")
    core = lax.axis_index("range")
    other = 1 - core
    first_row = pl.multiple_of(core * share, share)
    other_row = pl.multiple_of(other * share, share)
    halves = [lax.rem(aper // 2**level, 2) for level in range(levels)]
    partners = [aper + (1 - 2 * halves[level]) * 2**level for level in range(levels)]

    barrier = pltpu.get_barrier_semaphore()
    for partner in partners:
        pl.semaphore_signal(barrier, inc=1, device_id=(scene, partner, core), device_id_type=MESH)
    pl.semaphore_signal(barrier, inc=1, device_id=(scene, aper, other), device_id_type=MESH)

    local_copies = [
        pltpu.make_async_copy(
            matrix.at[pl.ds(half * angles + first_row, share), :],
            rows_of.at[half],
            local_sem.at[half],
        )
        for half in range(2)
    ]
    for copy in local_copies:
        copy.start()

    own_range = pl.ds(pl.multiple_of(core * span, span), span)
    for part in range(2):
        image[0, part, own_range, :] = images[0, part].T

    for level in range(levels):
        picked = pl.ds(pl.multiple_of(halves[level] * angles + core * share, LANES), share)
        index = tap_index[level, :, picked]
        weights = [jnp.zeros(index.shape, F32) for _ in range(taps)]
        for entry in range(tap_table.shape[1]):
            hit = index == entry
            for tap in range(taps):
                weights[tap] = jnp.where(hit, tap_table[tap, entry], weights[tap])
        lines = weights + [
            offsets[level, :, picked].astype(F32) + float(REACH - 3),
            phase_base[level, :, picked],
            phase_slope[level, :, picked],
        ]
        for row, line in enumerate(lines):
            for slot in range(2):
                role = halves[level] if slot == 0 else 1 - halves[level]
                params[level, slot, row : row + 1, :] = jnp.where(
                    role == 0, line[0:1], line[1:2]
                )
        edge = jnp.zeros((2, REACH, share), BF16)
        for buffer in (incoming, kept):
            buffer[level, :, 0:REACH, :] = edge
            buffer[level, :, REACH + width : REACH + width + REACH, :] = edge

    pl.semaphore_wait(barrier, len(partners) + 1)

    def first_copy(place):
        return pltpu.make_async_remote_copy(
            src_ref=image.at[0, :, place, :],
            dst_ref=image.at[0, :, place, :],
            send_sem=first_sem.at[0],
            recv_sem=first_sem.at[1],
            device_id=(scene, aper, other),
            device_id_type=MESH,
        )

    def inter_copy(level, step):
        return pltpu.make_async_remote_copy(
            src_ref=outgoing.at[level, :, pl.ds(pl.multiple_of(step * REACH, REACH), REACH), :],
            dst_ref=incoming.at[
                level, :, pl.ds(pl.multiple_of((step + 1) * REACH, REACH), REACH), :
            ],
            send_sem=inter_sem.at[0, level, step],
            recv_sem=inter_sem.at[1, level, step],
            device_id=(scene, partners[level], core),
            device_id_type=MESH,
        )

    def merge_copy(level, step, row):
        place = image.at[
            level, :, pl.ds(pl.multiple_of(step * REACH, REACH), REACH), pl.ds(row, share)
        ]
        return pltpu.make_async_remote_copy(
            src_ref=place,
            dst_ref=place,
            send_sem=merge_sem.at[0, level - 1, step],
            recv_sem=merge_sem.at[1, level - 1, step],
            device_id=(scene, aper, other),
            device_id_type=MESH,
        )

    def last_copy(row):
        return pltpu.make_async_remote_copy(
            src_ref=handed,
            dst_ref=out.at[0, :, pl.ds(row, share), :],
            send_sem=last_sem.at[0],
            recv_sem=last_sem.at[1],
            device_id=(scene, aper, other),
            device_id_type=MESH,
        )

    def send(level, step):
        if level > 0:
            merge_copy(level, step, other_row).wait_recv()
        here = pl.ds(pl.multiple_of(step * REACH, REACH), REACH)
        there = pl.ds(pl.multiple_of((step + 1) * REACH, REACH), REACH)
        both = jnp.concatenate([image[level, part, here, :] for part in range(2)], axis=0)
        for slot in range(2):
            half = 1 - halves[level] if slot == 0 else halves[level]
            inter = lax.dot_general(
                both, rows_of[half], (((1,), (1,)), ((), ())), preferred_element_type=F32
            ).astype(BF16)
            for part in range(2):
                piece = inter[part * REACH : (part + 1) * REACH]
                if slot == 0:
                    outgoing[level, part, here, :] = piece
                else:
                    kept[level, part, there, :] = piece
            if slot == 0:
                inter_copy(level, step).start()

    def term(level, slot, step, tile):
        buffer = kept if slot == 0 else incoming
        columns = slice(tile * LANES, (tile + 1) * LANES)

        def line(row, count):
            return jnp.broadcast_to(params[level, slot, row : row + 1, columns], (count, LANES))

        amount = line(taps, 2 * REACH).astype(jnp.int32)
        weights = [line(tap, REACH) for tap in range(taps)]
        order = lax.broadcasted_iota(jnp.int32, (REACH, LANES), 0) + step * REACH
        sine, cosine = sincos(
            line(taps + 1, REACH) + line(taps + 2, REACH) * order.astype(F32)
        )
        shifted = []
        for part in range(2):
            value = buffer[
                level, part, pl.ds(pl.multiple_of(step * REACH, REACH), 3 * REACH), columns
            ].astype(F32)
            keep = 2 * REACH
            bit = REACH
            value = jnp.concatenate(
                [
                    jnp.where((amount & bit) == bit, value[bit:], value[:keep]),
                    value[keep : keep + FINE],
                ],
                axis=0,
            )
            while bit > FINE:
                bit //= 2
                keep = value.shape[0] - bit
                value = jnp.where((amount[:keep] & bit) == bit, value[bit:], value[:keep])
            while bit > 1:
                bit //= 2
                turned = pltpu.roll(value, value.shape[0] - bit, 0)
                value = jnp.where((amount[: value.shape[0]] & bit) == bit, turned, value)
            window = windows.at[tile, slot, part]
            window[...] = value
            total = weights[0] * value[:REACH]
            for tap in range(1, taps):
                total = total + weights[tap] * window[tap : tap + REACH, :]
            shifted.append(total)
        return (
            shifted[0] * cosine - shifted[1] * sine,
            shifted[0] * sine + shifted[1] * cosine,
        )

    def merge(level, step):
        @pl.when(step == 0)
        def _():
            inter_copy(level, 0).wait_recv()

        @pl.when(step + 1 < steps)
        def _():
            inter_copy(level, step + 1).wait_recv()

        here = pl.ds(pl.multiple_of(step * REACH, REACH), REACH)
        for tile in range(tiles):
            terms = [term(level, slot, step, tile) for slot in range(2)]
            for part in range(2):
                total = terms[0][part] + terms[1][part]
                if level + 1 < levels:
                    columns = pl.ds(pl.multiple_of(first_row + tile * LANES, LANES), LANES)
                    image[level + 1, part, here, columns] = total.astype(BF16)
                else:
                    merged[part, here, tile * LANES : (tile + 1) * LANES] = total
        if level + 1 < levels:
            merge_copy(level + 1, step, first_row).start()
        else:

            @pl.when(lax.rem(step, per_owner) == per_owner - 1)
            def _():
                owner = step // per_owner
                block = pl.ds(pl.multiple_of(owner * span, span), span)

                @pl.when(owner == core)
                def _():
                    for part in range(2):
                        out[0, part, pl.ds(first_row, share), :] = merged[part, block, :].T.astype(BF16)

                @pl.when(owner != core)
                def _():
                    for part in range(2):
                        handed[part] = merged[part, block, :].T.astype(BF16)
                    last_copy(first_row).start()

    first = first_copy(own_range)
    first.start()
    for copy in local_copies:
        copy.wait()
    first.wait_send()
    first_copy(pl.ds(pl.multiple_of(other * span, span), span)).wait_recv()

    @pl.loop(0, steps)
    def _(step):
        send(0, step)

    stages = [(merge, 0, 0)]
    lag = 0
    for level in range(1, levels):
        lag += SEND_LAG
        stages.append((send, level, lag))
        lag += MERGE_LAG - SEND_LAG
        stages.append((merge, level, lag))

    @pl.loop(0, steps + lag)
    def _(tick):
        for stage, level, late in stages:

            @pl.when((tick >= late) & (tick < late + steps))
            def _():
                stage(level, tick - late)

    @pl.loop(0, steps)
    def _(step):
        for level in range(levels):
            inter_copy(level, step).wait_send()
            if level > 0:
                merge_copy(level, step, first_row).wait_send()

    last = last_copy(first_row)
    last.wait_send()
    last_copy(other_row).wait_recv()


def body(images, interp_matrix, offsets, tap_index, tap_table, phase_base, phase_slope):
    cores = lax.axis_size("range")
    levels = offsets.shape[0]
    angles = images.shape[2]
    span = images.shape[3]
    width = span * cores
    share = angles // cores
    steps = width // REACH
    vmem = pl.BlockSpec(memory_space=pltpu.VMEM)
    anywhere = pl.BlockSpec(memory_space=pl.ANY)
    framed = width + 2 * REACH
    return pl.pallas_call(
        functools.partial(kernel, levels),
        out_shape=pltpu.VMEM(images.shape, images.dtype),
        in_specs=[
            vmem,
            anywhere,
            vmem,
            vmem,
            pl.BlockSpec(memory_space=pltpu.SMEM),
            vmem,
            vmem,
        ],
        out_specs=vmem,
        scratch_shapes=[
            pltpu.VMEM((levels, 2, width, angles), BF16),
            pltpu.VMEM((2, share, angles), BF16),
            pltpu.VMEM((levels, 2, 16, share), F32),
            pltpu.VMEM((levels, 2, width, share), BF16),
            pltpu.VMEM((levels, 2, framed, share), BF16),
            pltpu.VMEM((levels, 2, framed, share), BF16),
            pltpu.VMEM((share // LANES, 2, 2, REACH + 2 * FINE, LANES), F32),
            pltpu.VMEM((2, width, share), F32),
            pltpu.VMEM((2, share, span), BF16),
            pltpu.SemaphoreType.DMA((2,)),
            pltpu.SemaphoreType.DMA((2,)),
            pltpu.SemaphoreType.DMA((2, levels, steps)),
            pltpu.SemaphoreType.DMA((2, levels - 1, steps)),
            pltpu.SemaphoreType.DMA((2,)),
        ],
        compiler_params=pltpu.CompilerParams(collective_id=0, has_side_effects=True),
    )(images, interp_matrix, offsets, tap_index, tap_table.T, phase_base, phase_slope)


def solution(mesh):
    return jax.shard_map(
        body,
        mesh=mesh,
        in_specs=(P(("scene", "aper"), None, None, "range"), P(), P(), P(), P(), P(), P()),
        out_specs=P(("scene", "aper"), None, None, "range"),
        check_vma=False,
    )
```

profile of v0, /device:TPU:0, one launch (start us, length us, event | category | flops | bytes accessed | tf_op | source)
XLA Modules:
  0.0 34.5 jit_solution(17510206439810910842)
XLA Ops:
  0.0 33.8 %shard_map.73 = bf16[1,2,512,128]{3,2,1,0:T(8,128)(2,1)S(1)} custom-call(bf16[1,2,512,128]{3,2,1,0:T(8,128)(2,1)} %images.1, bf16[1024,512]{1,0:T(8,128)(2,1)} %matrix.1, s32[3,2,1024]{2,1,0:T(2,128)} %offsets.1, s32[3,2,1024]{2,1,0:T(2,128)} %tap_index.1, f32[8,16]{1,0:T(8,128)} %bitcast.1, f32[3,2,1024]{2,1,0:T(2,128)} %phase_base.1, f32[3,2,1024]{2,1,0:T(2,128)} %phase_slope.1), custom_call_target="tpu_custom_call" | custom-call | tf_op jit(solution)/shard_map/pallas_call | solution.py:329
  33.8 0.7 %copy.9 = bf16[1,2,512,128]{3,2,1,0:T(8,128)(2,1)} copy(bf16[1,2,512,128]{3,2,1,0:T(8,128)(2,1)S(1)} %shard_map.73) | data formatting | bytes 524288
where the time goes:
time: 34.7 us; the launch traced here: 34.5 us
  Pallas kernels  33.8 us (97%)
  local copies, waits for them, and re-layouts  0.71 us (2%)
    pallas_call x1, Pallas kernels, body(): pl.pallas_call(functools.partial(kernel, levels), out_shape=pltpu.VMEM(im...  33.8 us
    unnamed x1, local copies, waits for them, and re-layouts  0.71 us

commit v1 on v0

--- a/solution.py
+++ b/solution.py
@@ -11,8 +11,8 @@
 LANES = 128
 REACH = 32
 FINE = 8
-SEND_LAG = 1
-MERGE_LAG = 5
+SEND_LAGS = (0, 1, 8)
+MERGE_LAGS = (0, 7, 17)
 F32 = jnp.float32
 BF16 = jnp.bfloat16
 
@@ -40,17 +40,25 @@
 
 def kernel(
     levels,
+    images_in,
+    matrix,
+    offsets_in,
+    tap_index_in,
+    tap_table,
+    phase_base_in,
+    phase_slope_in,
+    out,
     images,
-    matrix,
     offsets,
     tap_index,
-    tap_table,
     phase_base,
     phase_slope,
-    out,
+    source,
     image,
     rows_of,
     params,
+    trig,
+    staging,
     outgoing,
     incoming,
     kept,
@@ -59,14 +67,16 @@
     handed,
     local_sem,
     first_sem,
+    sibling_sem,
     inter_sem,
     merge_sem,
     last_sem,
 ):
     width = image.shape[2]
     angles = image.shape[3]
-    span = images.shape[3]
+    span = images.shape[2]
     share = rows_of.shape[1]
+    cores = angles // share
     tiles = share // LANES
     steps = width // REACH
     per_owner = span // REACH
@@ -85,72 +95,156 @@
         pl.semaphore_signal(barrier, inc=1, device_id=(scene, partner, core), device_id_type=MESH)
     pl.semaphore_signal(barrier, inc=1, device_id=(scene, aper, other), device_id_type=MESH)
 
+    pl.semaphore_signal(
+        barrier, inc=1, device_id=(scene, partners[0], other), device_id_type=MESH
+    )
+
     local_copies = [
-        pltpu.make_async_copy(
-            matrix.at[pl.ds(half * angles + first_row, share), :],
-            rows_of.at[half],
-            local_sem.at[half],
-        )
-        for half in range(2)
+        pltpu.make_async_copy(images_in.at[0], images, local_sem.at[0]),
+        pltpu.make_async_copy(matrix, rows_of, local_sem.at[1]),
+        pltpu.make_async_copy(offsets_in, offsets, local_sem.at[2]),
+        pltpu.make_async_copy(tap_index_in, tap_index, local_sem.at[3]),
+        pltpu.make_async_copy(phase_base_in, phase_base, local_sem.at[4]),
+        pltpu.make_async_copy(phase_slope_in, phase_slope, local_sem.at[5]),
     ]
     for copy in local_copies:
         copy.start()
 
-    own_range = pl.ds(pl.multiple_of(core * span, span), span)
+    def frame(step):
+        return pl.ds(pl.multiple_of((step + 1) * REACH, REACH), REACH)
+
+    def plain(step):
+        return pl.ds(pl.multiple_of(step * REACH, REACH), REACH)
+
+    def owner_of(step):
+        return step // per_owner
+
+    def local_step(step):
+        return lax.rem(step, per_owner)
+
+    def sibling_copy(step):
+        return pltpu.make_async_remote_copy(
+            src_ref=staging.at[0, :, plain(local_step(step)), :],
+            dst_ref=kept.at[0, :, frame(step), :],
+            send_sem=sibling_sem.at[0, step],
+            recv_sem=sibling_sem.at[1, step],
+            device_id=(scene, aper, other),
+            device_id_type=MESH,
+        )
+
+    def first_copy(step, place):
+        return pltpu.make_async_remote_copy(
+            src_ref=staging.at[1 + place, :, plain(local_step(step)), :],
+            dst_ref=incoming.at[0, :, frame(step), :],
+            send_sem=first_sem.at[place, local_step(step)],
+            recv_sem=inter_sem.at[1, 0, step],
+            device_id=(scene, partners[0], core if place == 0 else other),
+            device_id_type=MESH,
+        )
+
+    def inter_copy(level, step):
+        return pltpu.make_async_remote_copy(
+            src_ref=outgoing.at[level - 1, :, plain(step), :],
+            dst_ref=incoming.at[level, :, frame(step), :],
+            send_sem=inter_sem.at[0, level, step],
+            recv_sem=inter_sem.at[1, level, step],
+            device_id=(scene, partners[level], core),
+            device_id_type=MESH,
+        )
+
+    def product(both, row):
+        return lax.dot_general(
+            both, row, (((1,), (1,)), ((), ())), preferred_element_type=F32
+        ).astype(BF16)
+
+    def first_products(j):
+        step = core * per_owner + j
+        both = jnp.concatenate([source[part, plain(j), :] for part in range(2)], axis=0)
+        mine = halves[0] * cores
+        yours = (1 - halves[0]) * cores
+        for place, block in enumerate((mine + other, yours + core, yours + other)):
+            inter = product(both, rows_of[block])
+            for part in range(2):
+                staging[place, part, plain(j), :] = inter[part * REACH : (part + 1) * REACH]
+        inter = product(both, rows_of[mine + core])
+        for part in range(2):
+            kept[0, part, frame(step), :] = inter[part * REACH : (part + 1) * REACH]
+
+    local_copies[0].wait()
     for part in range(2):
-        image[0, part, own_range, :] = images[0, part].T
-
+        source[part] = images[part].T
+    local_copies[1].wait()
+    first_products(0)
+    edge = jnp.zeros((2, REACH, share), BF16)
     for level in range(levels):
-        picked = pl.ds(pl.multiple_of(halves[level] * angles + core * share, LANES), share)
+        for buffer in (incoming, kept):
+            buffer[level, :, 0:REACH, :] = edge
+            buffer[level, :, REACH + width : REACH + width + REACH, :] = edge
+
+    pl.semaphore_wait(barrier, len(partners) + 2)
+
+    @pl.loop(0, per_owner)
+    def _(j):
+        step = core * per_owner + j
+
+        @pl.when(j > 0)
+        def _():
+            first_products(j)
+
+        sibling_copy(step).start()
+
+        @pl.when(core == 0)
+        def _():
+            for place in range(2):
+                first_copy(step, place).start()
+
+    for copy in local_copies[2:]:
+        copy.wait()
+
+    def tables(level):
+        half = halves[level]
+        picked = pl.ds(pl.multiple_of(half * angles + core * share, LANES), share)
         index = tap_index[level, :, picked]
         weights = [jnp.zeros(index.shape, F32) for _ in range(taps)]
         for entry in range(tap_table.shape[1]):
             hit = index == entry
             for tap in range(taps):
                 weights[tap] = jnp.where(hit, tap_table[tap, entry], weights[tap])
-        lines = weights + [
-            offsets[level, :, picked].astype(F32) + float(REACH - 3),
-            phase_base[level, :, picked],
-            phase_slope[level, :, picked],
-        ]
+        base = phase_base[level, :, picked]
+        slope = phase_slope[level, :, picked]
+        lines = weights + [offsets[level, :, picked].astype(F32) + float(REACH - 3), base, slope]
         for row, line in enumerate(lines):
             for slot in range(2):
-                role = halves[level] if slot == 0 else 1 - halves[level]
-                params[level, slot, row : row + 1, :] = jnp.where(
-                    role == 0, line[0:1], line[1:2]
-                )
-        edge = jnp.zeros((2, REACH, share), BF16)
-        for buffer in (incoming, kept):
-            buffer[level, :, 0:REACH, :] = edge
-            buffer[level, :, REACH + width : REACH + width + REACH, :] = edge
-
-    pl.semaphore_wait(barrier, len(partners) + 1)
-
-    def first_copy(place):
-        return pltpu.make_async_remote_copy(
-            src_ref=image.at[0, :, place, :],
-            dst_ref=image.at[0, :, place, :],
-            send_sem=first_sem.at[0],
-            recv_sem=first_sem.at[1],
-            device_id=(scene, aper, other),
-            device_id_type=MESH,
-        )
-
-    def inter_copy(level, step):
-        return pltpu.make_async_remote_copy(
-            src_ref=outgoing.at[level, :, pl.ds(pl.multiple_of(step * REACH, REACH), REACH), :],
-            dst_ref=incoming.at[
-                level, :, pl.ds(pl.multiple_of((step + 1) * REACH, REACH), REACH), :
-            ],
-            send_sem=inter_sem.at[0, level, step],
-            recv_sem=inter_sem.at[1, level, step],
-            device_id=(scene, partners[level], core),
-            device_id_type=MESH,
-        )
+                role = half if slot == 0 else 1 - half
+                params[level, slot, row : row + 1, :] = jnp.where(role == 0, line[0:1], line[1:2])
+        for slot in range(2):
+            for tile in range(tiles):
+                columns = slice(tile * LANES, (tile + 1) * LANES)
+
+                def line(row, count):
+                    return jnp.broadcast_to(
+                        params[level, slot, row : row + 1, columns], (count, LANES)
+                    )
+
+                fine = lax.broadcasted_iota(jnp.int32, (REACH, LANES), 0).astype(F32)
+                coarse = (
+                    lax.broadcasted_iota(jnp.int32, (steps, LANES), 0) * REACH
+                ).astype(F32)
+                near = sincos(line(taps + 2, REACH) * fine)
+                far = sincos(line(taps + 1, steps) + line(taps + 2, steps) * coarse)
+                for step in range(steps):
+                    sine = jnp.broadcast_to(far[0][step : step + 1], (REACH, LANES))
+                    cosine = jnp.broadcast_to(far[1][step : step + 1], (REACH, LANES))
+                    place = pl.ds(step * REACH, REACH)
+                    trig[level, slot, 0, place, columns] = sine * near[1] + cosine * near[0]
+                    trig[level, slot, 1, place, columns] = cosine * near[1] - sine * near[0]
+
+    for level in range(levels):
+        tables(level)
 
     def merge_copy(level, step, row):
         place = image.at[
-            level, :, pl.ds(pl.multiple_of(step * REACH, REACH), REACH), pl.ds(row, share)
+            level - 1, :, pl.ds(pl.multiple_of(step * REACH, REACH), REACH), pl.ds(row, share)
         ]
         return pltpu.make_async_remote_copy(
             src_ref=place,
@@ -172,22 +266,18 @@
         )
 
     def send(level, step):
-        if level > 0:
-            merge_copy(level, step, other_row).wait_recv()
-        here = pl.ds(pl.multiple_of(step * REACH, REACH), REACH)
-        there = pl.ds(pl.multiple_of((step + 1) * REACH, REACH), REACH)
-        both = jnp.concatenate([image[level, part, here, :] for part in range(2)], axis=0)
+        merge_copy(level, step, other_row).wait_recv()
+        here = plain(step)
+        both = jnp.concatenate([image[level - 1, part, here, :] for part in range(2)], axis=0)
         for slot in range(2):
             half = 1 - halves[level] if slot == 0 else halves[level]
-            inter = lax.dot_general(
-                both, rows_of[half], (((1,), (1,)), ((), ())), preferred_element_type=F32
-            ).astype(BF16)
+            inter = product(both, rows_of[half * cores + core])
             for part in range(2):
                 piece = inter[part * REACH : (part + 1) * REACH]
                 if slot == 0:
-                    outgoing[level, part, here, :] = piece
+                    outgoing[level - 1, part, here, :] = piece
                 else:
-                    kept[level, part, there, :] = piece
+                    kept[level, part, frame(step), :] = piece
             if slot == 0:
                 inter_copy(level, step).start()
 
@@ -200,10 +290,7 @@
 
         amount = line(taps, 2 * REACH).astype(jnp.int32)
         weights = [line(tap, REACH) for tap in range(taps)]
-        order = lax.broadcasted_iota(jnp.int32, (REACH, LANES), 0) + step * REACH
-        sine, cosine = sincos(
-            line(taps + 1, REACH) + line(taps + 2, REACH) * order.astype(F32)
-        )
+        sine, cosine = [trig[level, slot, which, plain(step), columns] for which in range(2)]
         shifted = []
         for part in range(2):
             value = buffer[
@@ -238,13 +325,25 @@
         )
 
     def merge(level, step):
-        @pl.when(step == 0)
-        def _():
-            inter_copy(level, 0).wait_recv()
+        def arrive(at):
+            if level > 0:
+                inter_copy(level, at).wait_recv()
+            else:
+                first_copy(at, 0).wait_recv()
+
+                @pl.when(owner_of(at) != core)
+                def _():
+                    sibling_copy(at).wait_recv()
+
+        if level > 0:
+
+            @pl.when(step == 0)
+            def _():
+                arrive(0)
 
         @pl.when(step + 1 < steps)
         def _():
-            inter_copy(level, step + 1).wait_recv()
+            arrive(step + 1)
 
         here = pl.ds(pl.multiple_of(step * REACH, REACH), REACH)
         for tile in range(tiles):
@@ -253,7 +352,7 @@
                 total = terms[0][part] + terms[1][part]
                 if level + 1 < levels:
                     columns = pl.ds(pl.multiple_of(first_row + tile * LANES, LANES), LANES)
-                    image[level + 1, part, here, columns] = total.astype(BF16)
+                    image[level, part, here, columns] = total.astype(BF16)
                 else:
                     merged[part, here, tile * LANES : (tile + 1) * LANES] = total
         if level + 1 < levels:
@@ -276,24 +375,22 @@
                         handed[part] = merged[part, block, :].T.astype(BF16)
                     last_copy(first_row).start()
 
-    first = first_copy(own_range)
-    first.start()
-    for copy in local_copies:
-        copy.wait()
-    first.wait_send()
-    first_copy(pl.ds(pl.multiple_of(other * span, span), span)).wait_recv()
-
-    @pl.loop(0, steps)
-    def _(step):
-        send(0, step)
-
-    stages = [(merge, 0, 0)]
-    lag = 0
+    first_copy(0, 0).wait_recv()
+
+    @pl.when(core != 0)
+    def _():
+        sibling_copy(0).wait_recv()
+
+        @pl.loop(0, per_owner)
+        def _(j):
+            for place in range(2):
+                first_copy(core * per_owner + j, place).start()
+
+    stages = [(merge, 0, MERGE_LAGS[0])]
     for level in range(1, levels):
-        lag += SEND_LAG
-        stages.append((send, level, lag))
-        lag += MERGE_LAG - SEND_LAG
-        stages.append((merge, level, lag))
+        stages.append((send, level, SEND_LAGS[level]))
+        stages.append((merge, level, MERGE_LAGS[level]))
+    lag = MERGE_LAGS[levels - 1]
 
     @pl.loop(0, steps + lag)
     def _(tick):
@@ -305,10 +402,16 @@
 
     @pl.loop(0, steps)
     def _(step):
-        for level in range(levels):
+        for level in range(1, levels):
             inter_copy(level, step).wait_send()
-            if level > 0:
-                merge_copy(level, step, first_row).wait_send()
+            merge_copy(level, step, first_row).wait_send()
+
+    @pl.loop(0, per_owner)
+    def _(j):
+        step = core * per_owner + j
+        sibling_copy(step).wait_send()
+        for place in range(2):
+            first_copy(step, place).wait_send()
 
     last = last_copy(first_row)
     last.wait_send()
@@ -330,33 +433,42 @@
         functools.partial(kernel, levels),
         out_shape=pltpu.VMEM(images.shape, images.dtype),
         in_specs=[
-            vmem,
-            anywhere,
-            vmem,
-            vmem,
+            anywhere,
+            anywhere,
+            anywhere,
+            anywhere,
             pl.BlockSpec(memory_space=pltpu.SMEM),
-            vmem,
-            vmem,
+            anywhere,
+            anywhere,
         ],
         out_specs=vmem,
         scratch_shapes=[
-            pltpu.VMEM((levels, 2, width, angles), BF16),
-            pltpu.VMEM((2, share, angles), BF16),
+            pltpu.VMEM(images.shape[1:], images.dtype),
+            pltpu.VMEM(offsets.shape, offsets.dtype),
+            pltpu.VMEM(tap_index.shape, tap_index.dtype),
+            pltpu.VMEM(phase_base.shape, F32),
+            pltpu.VMEM(phase_slope.shape, F32),
+            pltpu.VMEM((2, span, angles), BF16),
+            pltpu.VMEM((levels - 1, 2, width, angles), BF16),
+            pltpu.VMEM((2 * cores, share, angles), BF16),
             pltpu.VMEM((levels, 2, 16, share), F32),
-            pltpu.VMEM((levels, 2, width, share), BF16),
+            pltpu.VMEM((levels, 2, 2, width, share), F32),
+            pltpu.VMEM((3, 2, span, share), BF16),
+            pltpu.VMEM((levels - 1, 2, width, share), BF16),
             pltpu.VMEM((levels, 2, framed, share), BF16),
             pltpu.VMEM((levels, 2, framed, share), BF16),
             pltpu.VMEM((share // LANES, 2, 2, REACH + 2 * FINE, LANES), F32),
             pltpu.VMEM((2, width, share), F32),
             pltpu.VMEM((2, share, span), BF16),
-            pltpu.SemaphoreType.DMA((2,)),
-            pltpu.SemaphoreType.DMA((2,)),
+            pltpu.SemaphoreType.DMA((6,)),
+            pltpu.SemaphoreType.DMA((2, steps // cores)),
+            pltpu.SemaphoreType.DMA((2, steps)),
             pltpu.SemaphoreType.DMA((2, levels, steps)),
             pltpu.SemaphoreType.DMA((2, levels - 1, steps)),
             pltpu.SemaphoreType.DMA((2,)),
         ],
         compiler_params=pltpu.CompilerParams(collective_id=0, has_side_effects=True),
-    )(images, interp_matrix, offsets, tap_index, tap_table.T, phase_base, phase_slope)
+    )(images, interp_matrix.reshape(2 * cores, share, angles), offsets, tap_index, tap_table.T, phase_base, phase_slope)
 
 
 def solution(mesh):

time: 34.7 us -> 35.3 us (1.017)
  Pallas kernels: 33.8 us -> 34.4 us
    pallas_call x1, Pallas kernels: 33.8 us -> 34.4 us  [body(): pl.pallas_call(functools.partial(kernel, levels), out_shape=pltpu.VMEM(im...]
where the time goes in v1:
time: 35.3 us; the launch traced here: 35.1 us
  Pallas kernels  34.4 us (97%)
  local copies, waits for them, and re-layouts  0.71 us (2%)
    pallas_call x1, Pallas kernels, body(): pl.pallas_call(functools.partial(kernel, levels), out_shape=pltpu.VMEM(im...  34.4 us

profile of v1, /device:TPU:0, one launch (start us, length us, event | category | flops | bytes accessed | tf_op | source)
XLA Modules:
  0.0 35.1 jit_solution(11872369765463546609)
XLA Ops:
  0.0 34.4 %shard_map.73 = bf16[1,2,512,128]{3,2,1,0:T(8,128)(2,1)S(1)} custom-call(bf16[1,2,512,128]{3,2,1,0:T(8,128)(2,1)} %images_in.1, bf16[4,256,512]{2,1,0:T(8,128)(2,1)} %bitcast.2, s32[3,2,1024]{2,1,0:T(2,128)} %offsets_in.1, s32[3,2,1024]{2,1,0:T(2,128)} %tap_index_in.1, f32[8,16]{1,0:T(8,128)} %bitcast.3, f32[3,2,1024]{2,1,0:T(2,128)} %phase_base_in.1, ...), custom_call_target="tpu_custom_call" | custom-call | tf_op jit(solution)/shard_map/pallas_call | solution.py:432
  34.4 0.7 %copy.9 = bf16[1,2,512,128]{3,2,1,0:T(8,128)(2,1)} copy(bf16[1,2,512,128]{3,2,1,0:T(8,128)(2,1)S(1)} %shard_map.73) | data formatting | bytes 524288

commit v2 on v1

--- a/solution.py
+++ b/solution.py
@@ -11,8 +11,11 @@
 LANES = 128
 REACH = 32
 FINE = 8
-SEND_LAGS = (0, 1, 8)
-MERGE_LAGS = (0, 7, 17)
+EARLY = 2
+LEADS = (0, 0, 0)
+COUNTS = (0, 1, 1)
+SEND_LAGS = (0, 1, 7)
+MERGE_LAGS = (0, 6, 16)
 F32 = jnp.float32
 BF16 = jnp.bfloat16
 
@@ -44,13 +47,14 @@
     matrix,
     offsets_in,
     tap_index_in,
-    tap_table,
+    tap_table_in,
     phase_base_in,
     phase_slope_in,
     out,
     images,
     offsets,
     tap_index,
+    tap_table,
     phase_base,
     phase_slope,
     source,
@@ -63,10 +67,10 @@
     incoming,
     kept,
     windows,
-    merged,
     handed,
+    assembled,
     local_sem,
-    first_sem,
+    sent_sem,
     sibling_sem,
     inter_sem,
     merge_sem,
@@ -106,6 +110,7 @@
         pltpu.make_async_copy(tap_index_in, tap_index, local_sem.at[3]),
         pltpu.make_async_copy(phase_base_in, phase_base, local_sem.at[4]),
         pltpu.make_async_copy(phase_slope_in, phase_slope, local_sem.at[5]),
+        pltpu.make_async_copy(tap_table_in, tap_table, local_sem.at[6]),
     ]
     for copy in local_copies:
         copy.start()
@@ -126,8 +131,8 @@
         return pltpu.make_async_remote_copy(
             src_ref=staging.at[0, :, plain(local_step(step)), :],
             dst_ref=kept.at[0, :, frame(step), :],
-            send_sem=sibling_sem.at[0, step],
-            recv_sem=sibling_sem.at[1, step],
+            send_sem=sent_sem.at[2 * levels],
+            recv_sem=sibling_sem.at[step],
             device_id=(scene, aper, other),
             device_id_type=MESH,
         )
@@ -136,8 +141,8 @@
         return pltpu.make_async_remote_copy(
             src_ref=staging.at[1 + place, :, plain(local_step(step)), :],
             dst_ref=incoming.at[0, :, frame(step), :],
-            send_sem=first_sem.at[place, local_step(step)],
-            recv_sem=inter_sem.at[1, 0, step],
+            send_sem=sent_sem.at[0],
+            recv_sem=inter_sem.at[0, step],
             device_id=(scene, partners[0], core if place == 0 else other),
             device_id_type=MESH,
         )
@@ -146,8 +151,8 @@
         return pltpu.make_async_remote_copy(
             src_ref=outgoing.at[level - 1, :, plain(step), :],
             dst_ref=incoming.at[level, :, frame(step), :],
-            send_sem=inter_sem.at[0, level, step],
-            recv_sem=inter_sem.at[1, level, step],
+            send_sem=sent_sem.at[level],
+            recv_sem=inter_sem.at[level, step],
             device_id=(scene, partners[level], core),
             device_id_type=MESH,
         )
@@ -174,7 +179,8 @@
     for part in range(2):
         source[part] = images[part].T
     local_copies[1].wait()
-    first_products(0)
+    for j in range(EARLY):
+        first_products(j)
     edge = jnp.zeros((2, REACH, share), BF16)
     for level in range(levels):
         for buffer in (incoming, kept):
@@ -187,7 +193,7 @@
     def _(j):
         step = core * per_owner + j
 
-        @pl.when(j > 0)
+        @pl.when(j >= EARLY)
         def _():
             first_products(j)
 
@@ -249,18 +255,18 @@
         return pltpu.make_async_remote_copy(
             src_ref=place,
             dst_ref=place,
-            send_sem=merge_sem.at[0, level - 1, step],
-            recv_sem=merge_sem.at[1, level - 1, step],
+            send_sem=sent_sem.at[levels + level - 1],
+            recv_sem=merge_sem.at[level - 1, step],
             device_id=(scene, aper, other),
             device_id_type=MESH,
         )
 
-    def last_copy(row):
+    def last_copy(step, row):
         return pltpu.make_async_remote_copy(
-            src_ref=handed,
-            dst_ref=out.at[0, :, pl.ds(row, share), :],
-            send_sem=last_sem.at[0],
-            recv_sem=last_sem.at[1],
+            src_ref=handed.at[:, plain(step), :],
+            dst_ref=assembled.at[:, plain(local_step(step)), pl.ds(row, share)],
+            send_sem=sent_sem.at[2 * levels - 1],
+            recv_sem=last_sem.at[step],
             device_id=(scene, aper, other),
             device_id_type=MESH,
         )
@@ -269,17 +275,12 @@
         merge_copy(level, step, other_row).wait_recv()
         here = plain(step)
         both = jnp.concatenate([image[level - 1, part, here, :] for part in range(2)], axis=0)
-        for slot in range(2):
-            half = 1 - halves[level] if slot == 0 else halves[level]
-            inter = product(both, rows_of[half * cores + core])
-            for part in range(2):
-                piece = inter[part * REACH : (part + 1) * REACH]
-                if slot == 0:
-                    outgoing[level - 1, part, here, :] = piece
-                else:
-                    kept[level, part, frame(step), :] = piece
-            if slot == 0:
-                inter_copy(level, step).start()
+        away = product(both, rows_of[(1 - halves[level]) * cores + core])
+        home = product(both, rows_of[halves[level] * cores + core])
+        for part in range(2):
+            outgoing[level - 1, part, here, :] = away[part * REACH : (part + 1) * REACH]
+            kept[level, part, frame(step), :] = home[part * REACH : (part + 1) * REACH]
+        inter_copy(level, step).start()
 
     def term(level, slot, step, tile):
         buffer = kept if slot == 0 else incoming
@@ -354,26 +355,23 @@
                     columns = pl.ds(pl.multiple_of(first_row + tile * LANES, LANES), LANES)
                     image[level, part, here, columns] = total.astype(BF16)
                 else:
-                    merged[part, here, tile * LANES : (tile + 1) * LANES] = total
+                    value = total.astype(BF16)
+
+                    @pl.when(owner_of(step) == core)
+                    def _():
+                        columns = pl.ds(pl.multiple_of(first_row + tile * LANES, LANES), LANES)
+                        assembled[part, plain(local_step(step)), columns] = value
+
+                    @pl.when(owner_of(step) != core)
+                    def _():
+                        handed[part, here, tile * LANES : (tile + 1) * LANES] = value
         if level + 1 < levels:
             merge_copy(level + 1, step, first_row).start()
         else:
 
-            @pl.when(lax.rem(step, per_owner) == per_owner - 1)
+            @pl.when(owner_of(step) != core)
             def _():
-                owner = step // per_owner
-                block = pl.ds(pl.multiple_of(owner * span, span), span)
-
-                @pl.when(owner == core)
-                def _():
-                    for part in range(2):
-                        out[0, part, pl.ds(first_row, share), :] = merged[part, block, :].T.astype(BF16)
-
-                @pl.when(owner != core)
-                def _():
-                    for part in range(2):
-                        handed[part] = merged[part, block, :].T.astype(BF16)
-                    last_copy(first_row).start()
+                last_copy(step, first_row).start()
 
     first_copy(0, 0).wait_recv()
 
@@ -396,26 +394,47 @@
     def _(tick):
         for stage, level, late in stages:
 
-            @pl.when((tick >= late) & (tick < late + steps))
+            lead = LEADS[level] if stage is send else 0
+
+            @pl.when((tick >= late - lead) & (tick < late + steps))
             def _():
-                stage(level, tick - late)
-
-    @pl.loop(0, steps)
-    def _(step):
-        for level in range(1, levels):
-            inter_copy(level, step).wait_send()
-            merge_copy(level, step, first_row).wait_send()
+                if stage is send:
+                    count = COUNTS[level]
+                    first = tick == late - LEADS[level]
+                    low = jnp.where(first, 0, jnp.maximum(count, tick - late))
+                    high = jnp.where(first, count, tick - late + 1)
+
+                    @pl.loop(low, high)
+                    def _(step):
+                        send(level, step)
+
+                else:
+                    stage(level, tick - late)
 
     @pl.loop(0, per_owner)
     def _(j):
-        step = core * per_owner + j
-        sibling_copy(step).wait_send()
-        for place in range(2):
-            first_copy(step, place).wait_send()
-
-    last = last_copy(first_row)
-    last.wait_send()
-    last_copy(other_row).wait_recv()
+        last_copy(core * per_owner + j, other_row).wait_recv()
+
+    for part in range(2):
+        out[0, part] = assembled[part].T
+
+    def all_sent(ref, sem):
+        pltpu.make_async_remote_copy(
+            src_ref=ref,
+            dst_ref=ref,
+            send_sem=sent_sem.at[sem],
+            recv_sem=last_sem.at[0],
+            device_id=(scene, aper, other),
+            device_id_type=MESH,
+        ).wait_send()
+
+    all_sent(staging.at[0], 2 * levels)
+    all_sent(staging.at[pl.ds(1, 2)], 0)
+    for level in range(1, levels):
+        all_sent(outgoing.at[level - 1], level)
+        all_sent(image.at[level - 1, :, :, pl.ds(first_row, share)], levels + level - 1)
+    theirs = pl.ds(pl.multiple_of(other * span, span), span)
+    all_sent(handed.at[:, theirs, :], 2 * levels - 1)
 
 
 def body(images, interp_matrix, offsets, tap_index, tap_table, phase_base, phase_slope):
@@ -437,7 +456,7 @@
             anywhere,
             anywhere,
             anywhere,
-            pl.BlockSpec(memory_space=pltpu.SMEM),
+            anywhere,
             anywhere,
             anywhere,
         ],
@@ -446,6 +465,7 @@
             pltpu.VMEM(images.shape[1:], images.dtype),
             pltpu.VMEM(offsets.shape, offsets.dtype),
             pltpu.VMEM(tap_index.shape, tap_index.dtype),
+            pltpu.SMEM(tap_table.shape[::-1], F32),
             pltpu.VMEM(phase_base.shape, F32),
             pltpu.VMEM(phase_slope.shape, F32),
             pltpu.VMEM((2, span, angles), BF16),
@@ -458,14 +478,14 @@
             pltpu.VMEM((levels, 2, framed, share), BF16),
             pltpu.VMEM((levels, 2, framed, share), BF16),
             pltpu.VMEM((share // LANES, 2, 2, REACH + 2 * FINE, LANES), F32),
-            pltpu.VMEM((2, width, share), F32),
-            pltpu.VMEM((2, share, span), BF16),
-            pltpu.SemaphoreType.DMA((6,)),
-            pltpu.SemaphoreType.DMA((2, steps // cores)),
-            pltpu.SemaphoreType.DMA((2, steps)),
-            pltpu.SemaphoreType.DMA((2, levels, steps)),
-            pltpu.SemaphoreType.DMA((2, levels - 1, steps)),
-            pltpu.SemaphoreType.DMA((2,)),
+            pltpu.VMEM((2, width, share), BF16),
+            pltpu.VMEM((2, span, angles), BF16),
+            pltpu.SemaphoreType.DMA((7,)),
+            pltpu.SemaphoreType.DMA((2 * levels + 1,)),
+            pltpu.SemaphoreType.DMA((steps,)),
+            pltpu.SemaphoreType.DMA((levels, steps)),
+            pltpu.SemaphoreType.DMA((levels - 1, steps)),
+            pltpu.SemaphoreType.DMA((steps,)),
         ],
         compiler_params=pltpu.CompilerParams(collective_id=0, has_side_effects=True),
     )(images, interp_matrix.reshape(2 * cores, share, angles), offsets, tap_index, tap_table.T, phase_base, phase_slope)

time: 35.3 us -> 33.1 us (0.938)
  Pallas kernels: 34.4 us -> 32.2 us
    pallas_call x1, Pallas kernels: 34.4 us -> 32.2 us  [body(): pl.pallas_call(functools.partial(kernel, levels), out_shape=pltpu.VMEM(im...]
where the time goes in v2:
time: 33.1 us; the launch traced here: 32.9 us
  Pallas kernels  32.2 us (97%)
  local copies, waits for them, and re-layouts  0.71 us (2%)
    pallas_call x1, Pallas kernels, body(): pl.pallas_call(functools.partial(kernel, levels), out_shape=pltpu.VMEM(im...  32.2 us
    unnamed x1, local copies, waits for them, and re-layouts  0.71 us

profile of v2, /device:TPU:0, one launch (start us, length us, event | category | flops | bytes accessed | tf_op | source)
XLA Modules:
  0.0 32.9 jit_solution(14630591236215627559)
XLA Ops:
  0.0 32.2 %shard_map.73 = bf16[1,2,512,128]{3,2,1,0:T(8,128)(2,1)S(1)} custom-call(bf16[1,2,512,128]{3,2,1,0:T(8,128)(2,1)} %images_in.1, bf16[4,256,512]{2,1,0:T(8,128)(2,1)} %bitcast.2, s32[3,2,1024]{2,1,0:T(2,128)} %offsets_in.1, s32[3,2,1024]{2,1,0:T(2,128)} %tap_index_in.1, f32[8,16]{1,0:T(8,128)} %bitcast.3, f32[3,2,1024]{2,1,0:T(2,128)} %phase_base_in.1, ...), custom_call_target="tpu_custom_call" | custom-call | tf_op jit(solution)/shard_map/pallas_call | solution.py:451
  32.2 0.7 %copy.9 = bf16[1,2,512,128]{3,2,1,0:T(8,128)(2,1)} copy(bf16[1,2,512,128]{3,2,1,0:T(8,128)(2,1)S(1)} %shard_map.73) | data formatting | bytes 524288

commit v3 on v2

--- a/solution.py
+++ b/solution.py
@@ -11,9 +11,12 @@
 LANES = 128
 REACH = 32
 FINE = 8
-EARLY = 2
+EARLY = 1
 LEADS = (0, 0, 0)
-COUNTS = (0, 1, 1)
+COUNTS = (0, 1, 0)
+PAIRED = ((False, True), (True, False), (False, False))
+SEND_FIRST = True
+WAIT_FIRST = True
 SEND_LAGS = (0, 1, 7)
 MERGE_LAGS = (0, 6, 16)
 F32 = jnp.float32
@@ -373,40 +376,57 @@
             def _():
                 last_copy(step, first_row).start()
 
-    first_copy(0, 0).wait_recv()
+    if WAIT_FIRST:
+        first_copy(0, 0).wait_recv()
 
     @pl.when(core != 0)
     def _():
-        sibling_copy(0).wait_recv()
-
         @pl.loop(0, per_owner)
         def _(j):
             for place in range(2):
                 first_copy(core * per_owner + j, place).start()
 
+        sibling_copy(0).wait_recv()
+
+    if not WAIT_FIRST:
+        first_copy(0, 0).wait_recv()
+
     stages = [(merge, 0, MERGE_LAGS[0])]
     for level in range(1, levels):
         stages.append((send, level, SEND_LAGS[level]))
-        stages.append((merge, level, MERGE_LAGS[level]))
+        if level > 1:
+            stages.append((merge, level - 1, MERGE_LAGS[level - 1]))
+    if SEND_FIRST:
+        stages = [(merge, 0, MERGE_LAGS[0])]
+        stages += [(send, level, SEND_LAGS[level]) for level in range(1, levels)]
+        stages += [(merge, level, MERGE_LAGS[level]) for level in range(1, levels - 1)]
+    stages.append((merge, levels - 1, MERGE_LAGS[levels - 1]))
     lag = MERGE_LAGS[levels - 1]
 
     @pl.loop(0, steps + lag)
     def _(tick):
         for stage, level, late in stages:
-
-            lead = LEADS[level] if stage is send else 0
+            sends = stage is send
+            lead = LEADS[level] if sends else 0
+            paired = PAIRED[level][0 if sends else 1]
 
             @pl.when((tick >= late - lead) & (tick < late + steps))
             def _():
-                if stage is send:
-                    count = COUNTS[level]
-                    first = tick == late - LEADS[level]
-                    low = jnp.where(first, 0, jnp.maximum(count, tick - late))
-                    high = jnp.where(first, count, tick - late + 1)
+                count = COUNTS[level] if sends else 0
+                first = tick == late - lead
+                low = jnp.maximum(count, tick - late)
+                high = tick - late + 1
+                if count:
+                    low = jnp.where(first, 0, low)
+                    high = jnp.where(first, count, high)
+                if paired:
+                    low = jnp.where(tick - late == steps - 1, steps, low)
+                    high = jnp.where(tick - late == steps - 2, steps, high)
+                if count or paired:
 
                     @pl.loop(low, high)
                     def _(step):
-                        send(level, step)
+                        stage(level, step)
 
                 else:
                     stage(level, tick - late)

time: 33.1 us -> 32.3 us (0.976)
  Pallas kernels: 32.2 us -> 31.5 us
    pallas_call x1, Pallas kernels: 32.2 us -> 31.5 us  [body(): pl.pallas_call(functools.partial(kernel, levels), out_shape=pltpu.VMEM(im...]
where the time goes in v3:
time: 32.3 us; the launch traced here: 32.2 us
  Pallas kernels  31.5 us (98%)
  local copies, waits for them, and re-layouts  0.71 us (2%)
    pallas_call x1, Pallas kernels, body(): pl.pallas_call(functools.partial(kernel, levels), out_shape=pltpu.VMEM(im...  31.5 us
    unnamed x1, local copies, waits for them, and re-layouts  0.71 us

profile of v3, /device:TPU:0, one launch (start us, length us, event | category | flops | bytes accessed | tf_op | source)
XLA Modules:
  0.0 32.2 jit_solution(133468145296788285)
XLA Ops:
  0.0 31.5 %shard_map.73 = bf16[1,2,512,128]{3,2,1,0:T(8,128)(2,1)S(1)} custom-call(bf16[1,2,512,128]{3,2,1,0:T(8,128)(2,1)} %images_in.1, bf16[4,256,512]{2,1,0:T(8,128)(2,1)} %bitcast.2, s32[3,2,1024]{2,1,0:T(2,128)} %offsets_in.1, s32[3,2,1024]{2,1,0:T(2,128)} %tap_index_in.1, f32[8,16]{1,0:T(8,128)} %bitcast.3, f32[3,2,1024]{2,1,0:T(2,128)} %phase_base_in.1, ...), custom_call_target="tpu_custom_call" | custom-call | tf_op jit(solution)/shard_map/pallas_call | solution.py:471
  31.5 0.7 %copy.9 = bf16[1,2,512,128]{3,2,1,0:T(8,128)(2,1)} copy(bf16[1,2,512,128]{3,2,1,0:T(8,128)(2,1)S(1)} %shard_map.73) | data formatting | bytes 524288

commit v4 on v3

--- a/solution.py
+++ b/solution.py
@@ -200,12 +200,12 @@
         def _():
             first_products(j)
 
-        sibling_copy(step).start()
-
         @pl.when(core == 0)
         def _():
             for place in range(2):
                 first_copy(step, place).start()
+
+        sibling_copy(step).start()
 
     for copy in local_copies[2:]:
         copy.wait()
@@ -431,12 +431,17 @@
                 else:
                     stage(level, tick - late)
 
+    def turn(row):
+        for part in range(2):
+            out[0, part, pl.ds(row, share), :] = assembled[part, :, pl.ds(row, share)].T
+
+    turn(first_row)
+
     @pl.loop(0, per_owner)
     def _(j):
         last_copy(core * per_owner + j, other_row).wait_recv()
 
-    for part in range(2):
-        out[0, part] = assembled[part].T
+    turn(other_row)
 
     def all_sent(ref, sem):
         pltpu.make_async_remote_copy(

time: 32.3 us -> 32.3 us (level)
  no operation moved by 1% of the time
where the time goes in v4:
time: 32.3 us; the launch traced here: 32.2 us
  Pallas kernels  31.5 us (98%)
  local copies, waits for them, and re-layouts  0.71 us (2%)
    pallas_call x1, Pallas kernels, body(): pl.pallas_call(functools.partial(kernel, levels), out_shape=pltpu.VMEM(im...  31.5 us
    unnamed x1, local copies, waits for them, and re-layouts  0.71 us

profile of v4, /device:TPU:0, one launch (start us, length us, event | category | flops | bytes accessed | tf_op | source)
XLA Modules:
  0.0 32.2 jit_solution(14331889669354424800)
XLA Ops:
  0.0 31.5 %shard_map.73 = bf16[1,2,512,128]{3,2,1,0:T(8,128)(2,1)S(1)} custom-call(bf16[1,2,512,128]{3,2,1,0:T(8,128)(2,1)} %images_in.1, bf16[4,256,512]{2,1,0:T(8,128)(2,1)} %bitcast.2, s32[3,2,1024]{2,1,0:T(2,128)} %offsets_in.1, s32[3,2,1024]{2,1,0:T(2,128)} %tap_index_in.1, f32[8,16]{1,0:T(8,128)} %bitcast.3, f32[3,2,1024]{2,1,0:T(2,128)} %phase_base_in.1, ...), custom_call_target="tpu_custom_call" | custom-call | tf_op jit(solution)/shard_map/pallas_call | solution.py:476
  31.5 0.7 %copy.9 = bf16[1,2,512,128]{3,2,1,0:T(8,128)(2,1)} copy(bf16[1,2,512,128]{3,2,1,0:T(8,128)(2,1)S(1)} %shard_map.73) | data formatting | bytes 524288
